TPU v7x, 32 devices: a whole 2x2x4 slice. The times are simulated.
32 devices in a mesh: band: 8 (over z, x), coef: 4 (over y, core).
Axes of the slice: x: 2, y: 2, z: 4, core: 2. Of those that a mesh axis runs over, the one named last changes fastest.
Arguments:
- coeffs: float32 [1024, 262144], P('band', 'coef'), may hold values from -320 to 320
- ref_block: float32 [1024, 262144], P('band', 'coef'), may hold values from -0.01171875 to 0.01171875
- index_map: int32 [262144], P('coef'), may hold values from 0 to 65535, as said below
- band_group: int32 [1024], P('band'), may hold values from 0 to 15
Outputs:
- ortho: float32 [1024, 262144], P('band', 'coef')
- band_residual: float32 [1024], P('band')
- group_residual: float32 [16], replicated
Inputs may be any that keep to these rules, and one draw needn't show every extreme that they name: Within each aligned slab of 65536 coefficients, index_map holds every number of 0 to 65535 once.
All inputs are finite; a program needn't handle non-finite values.
Results may differ from a plain program's by a relative error of at most 0.000098.
Values sent between devices are 32-bit elements; how exact they have to be, the bound alone decides.
A program may use at most 384 MiB of HBM per device.

v0:
```python
import jax
import jax.numpy as jnp
from jax import lax
from jax.sharding import PartitionSpec as P

NGROUPS = 16
BLOCK = 128
ROWS = 256


def high(a, b):
    return jnp.dot(a, b, precision=lax.Precision.HIGH, preferred_element_type=jnp.float32)


def highest(a, b):
    return jnp.dot(a, b, precision=lax.Precision.HIGHEST, preferred_element_type=jnp.float32)


def inverse_factor(margin):
    size = margin.shape[0]
    eye = jnp.eye(BLOCK, dtype=jnp.float32)
    rest = margin
    below = jnp.zeros((size, 0), jnp.float32)
    rows = []
    for start in range(0, size, BLOCK):
        corner = lax.linalg.cholesky(rest[:BLOCK, :BLOCK], symmetrize_input=False)
        inv = lax.linalg.triangular_solve(corner, eye, left_side=True, lower=True)
        row = jnp.concatenate([highest(inv, below[:BLOCK]), inv], axis=1) if start else inv
        rows.append(jnp.pad(row, ((0, 0), (0, size - row.shape[1]))))
        if start + BLOCK < size:
            panel = highest(rest[BLOCK:, :BLOCK], inv.T)
            change = highest(panel, row)
            below = jnp.pad(below[BLOCK:], ((0, 0), (0, BLOCK))) - change
            rest = rest[BLOCK:, BLOCK:] - highest(panel, panel.T)
    return jnp.concatenate(rows, axis=0)


def local(coeffs, ref_block, index_map, band_group):
    devices = lax.axis_size("band")
    bands, slab = coeffs.shape
    part = slab // devices
    total = bands * devices
    pieces = coeffs.reshape(bands, devices, part).transpose(1, 0, 2)
    columns = lax.all_to_all(pieces, "band", split_axis=0, concat_axis=0, tiled=True)
    columns = columns.reshape(total, part)
    _, inverse = lax.sort((index_map, jnp.arange(slab, dtype=jnp.int32)), num_keys=1)
    ref_own = jnp.take(ref_block, inverse, axis=1, unique_indices=True, mode="clip")
    tops = range(0, total, ROWS)
    strips = [high(columns[t : t + ROWS], columns[: t + ROWS].T) for t in tops]
    strips = lax.psum(jnp.concatenate(strips, axis=1), ("band", "coef"))
    lower, at = ([], 0)
    for t in tops:
        width = t + ROWS
        lower.append(jnp.pad(strips[:, at : at + width], ((0, 0), (0, total - width))))
        at += width
    lower = jnp.concatenate(lower, axis=0)
    low = jnp.tril(lower)
    margin = low + jnp.tril(lower, -1).T
    inv = inverse_factor(margin)
    ortho_cols = jnp.concatenate(
        [high(inv[t : t + ROWS, : t + ROWS], columns[: t + ROWS]) for t in tops], axis=0
    )
    back = lax.all_to_all(
        ortho_cols.reshape(devices, bands, part), "band", split_axis=0, concat_axis=0, tiled=True
    )
    ortho = back.transpose(1, 0, 2).reshape(bands, slab)
    squares = jnp.sum((ortho - ref_own) ** 2, axis=1)
    band_residual = jnp.sqrt(lax.psum(squares, "coef") + 1e-06)
    onehot = (band_group[:, None] == jnp.arange(NGROUPS, dtype=jnp.int32)[None, :]).astype(
        jnp.float32
    )
    terms = highest(band_residual, onehot)
    group_residual = lax.psum(terms, "band") * (NGROUPS / total)
    return (ortho, band_residual, group_residual)


def solution(mesh):
    return jax.shard_map(
        local,
        mesh=mesh,
        in_specs=(P("band", "coef"), P("band", "coef"), P("coef"), P("band")),
        out_specs=(P("band", "coef"), P("band"), P()),
        check_vma=False,
    )
```

profile of v0, /device:TPU:0, one launch (start us, length us, event | category | flops | bytes accessed | tf_op | source)
XLA Modules:
  0.0 2275.0 jit_solution(11808679882351079061)
XLA Ops:
  7.2 33.4 %copy.37 = f32[128,65536]{0,1:T(8,128)} copy(f32[128,65536]{1,0:T(8,128)} %param.7) | data formatting | bytes 67108864 | tf_op args[0]
  40.6 735.1 %all_to_all.10 = f32[8,128,8192]{1,2,0:T(8,128)} all-to-all(f32[8,128,8192]{1,2,0:T(8,128)} %bitcast.125), channel_id=1, replica_groups=mesh['band'=8,'coef'=4] {'band'}, dimensions={0} | all-to-all | bytes 67108864 | tf_op jit(solution)/shard_map/all_to_all | solution.py:44
  775.7 23.5 %fusion.100 = (f32[2,128,8192]{1,2,0:T(8,128)}, f32[2,128,8192]{1,2,0:T(8,128)}, f32[2,128,8192]{1,2,0:T(8,128)}, f32[2,128,8192]{1,2,0:T(8,128)}) fusion(f32[8,128,8192]{1,2,0:T(8,128)} %all_to_all.10), kind=kLoop, calls=%fused_computation.177 | loop fusion | bytes 67108864 | tf_op jit(solution)/shard_map/slice | solution.py:49
  808.2 16.9 slice.228
  825.1 24.7 %copy.42 = f32[6,128,8192]{2,1,0:T(8,128)} copy(f32[6,128,8192]{1,2,0:T(8,128)} %slice.228) | data formatting | bytes 50331648 | tf_op jit(solution)/shard_map/slice | solution.py:49
  870.2 17.5 copy.40
  905.5 14.1 fusion.101
  919.5 22.3 fusion.103
  941.8 12.9 fusion.102
  954.8 31.1 %copy.44 = f32[8,128,8192]{2,1,0:T(8,128)} copy(f32[8,128,8192]{1,2,0:T(8,128)} %all_to_all.10) | data formatting | bytes 67108864 | tf_op jit(solution)/shard_map/all_to_all | solution.py:44
  985.9 19.7 fusion.104
  1007.3 135.5 %all-reduce.17.cloned.1.call-done = f32[256,2560]{0,1:T(8,128)} async-done(((f32[256,2560]{0,1:T(8,128)}), f32[256,2560]{0,1:T(8,128)}) %all-reduce.17.cloned.1.call-update) | async-done | bytes 2621456 | tf_op jit(solution)/shard_map/psum | solution.py:50
  1389.8 13.1 fusion.17
  1402.9 18.0 fusion.12
  1420.9 23.5 %fusion.6 = f32[256,8192]{1,0:T(8,128)} fusion(f32[1024,8192]{1,0:T(8,128)} %bitcast.119, f32[128,896]{1,0:T(8,128)S(1)} %pad_maximum_fusion.2, f32[128,128]{1,0:T(8,128)S(1)} %copy.56, f32[128,896]{1,0:T(8,128)S(1)} %fusion.105), kind=kOutput, calls=%fused_computation.35 | convolution fusion | flops 12885950464 | bytes 42926080 | tf_op jit(solution)/shard_map/dot_general | solution.py:12
  1444.4 23.6 %pad_maximum_fusion = f32[1024,8192]{1,0:T(8,128)} fusion(f32[256,8192]{1,0:T(8,128)} %fusion.6, f32[256,8192]{1,0:T(8,128)} %fusion.12, f32[256,8192]{1,0:T(8,128)} %fusion.17, f32[256,8192]{1,0:T(8,128)} %fusion.38), kind=kLoop, calls=%fused_computation.1 | loop fusion | flops 25165824 | bytes 67108864 | tf_op jit(solution)/shard_map/concatenate | solution.py:60
  1475.3 33.4 %copy.58 = f32[128,65536]{0,1:T(8,128)} copy(f32[128,65536]{1,0:T(8,128)} %param.8) | data formatting | bytes 67108864 | tf_op args[1]
  1508.8 25.5 %sort.15 = (s32[65536]{0:T(1024)}, s32[65536]{0:T(1024)S(1)}) sort(s32[65536]{0:T(1024)S(1)} %copy-done.5, s32[65536]{0:T(1024)S(1)} %iota.166), dimensions={0}, to_apply=%region_3.6 | sort | flops 1048576 | bytes 1048576 | tf_op jit(solution)/shard_map/sort | solution.py:46
  1534.3 226.1 %gather_fusion = f32[65536,128]{1,0:T(8,128)} fusion(f32[128,65536]{0,1:T(8,128)} %copy.58, s32[65536]{0:T(1024)S(1)} %broadcast_clamp_fusion), kind=kCustom, calls=%fused_computation | custom fusion | bytes 67371008 | tf_op jit(solution)/shard_map/jit(_take)/gather | solution.py:47
  1760.4 31.1 %copy.59 = f32[128,8,8192]{2,0,1:T(8,128)} copy(f32[128,8,8192]{0,2,1:T(8,128)} %bitcast.128) | data formatting | bytes 67108864 | tf_op jit(solution)/shard_map/jit(_take)/gather | solution.py:47
  1791.5 405.6 %all-to-all-done.1 = f32[8,128,8192]{2,1,0:T(8,128)} async-done(((f32[8,128,8192]{2,1,0:T(8,128)}), f32[8,128,8192]{2,1,0:T(8,128)}, u32[]{:S(2)}, u32[]{:S(2)}) %all-to-all-start.1) | async-done | bytes 33554464 | tf_op jit(solution)/shard_map/all_to_all | solution.py:63
  2197.1 20.9 fusion.1
  2223.8 20.4 psum.23
  2244.8 22.9 %copy.64 = f32[8,16,8,8192]{3,2,0,1:T(8,128)} copy(f32[8,16,8,8192]{3,2,1,0:T(8,128)} %bitcast.34) | data formatting | bytes 67108864 | tf_op jit(solution)/shard_map/reshape | solution.py:66
  (143 shorter events, 308.8 us)
Async XLA Ops:
  7.2 1135.6 %all-reduce.17.cloned.1.call-start = ((), (), s32[]{:S(2)}) async-start(), calls=%async_computation.2 | async-start | bytes 5242880 | tf_op jit(solution)/shard_map/psum | solution.py:50
  1005.5 139.5 %copy-start.6 = (pred[1024]{0:T(1024)(128)(4,1)S(1)}, pred[1024]{0:T(1024)(128)(4,1)}, u32[]{:S(2)}) copy-start(pred[1024]{0:T(1024)(128)(4,1)} %constant.30.clone.1) | copy-start | bytes 3076
  1158.7 1.9 copy-start
  1219.3 1.5 copy-start.1
  1302.4 23.7 %copy-start.2 = (f32[384,384]{1,0:T(8,128)}, f32[384,384]{1,0:T(8,128)S(1)}, u32[]{:S(2)}) copy-start(f32[384,384]{1,0:T(8,128)S(1)} %convolution_subtract_fusion.6) | copy-start | bytes 1769476
  1354.2 35.4 %copy-start.3 = (f32[128,512]{1,0:T(8,128)S(1)}, f32[128,512]{1,0:T(8,128)}, u32[]{:S(2)}) copy-start(f32[128,512]{1,0:T(8,128)} %pad_maximum_fusion.5) | copy-start | bytes 786436
  1354.2 35.6 %copy-start.4 = (f32[128,384]{1,0:T(8,128)S(1)}, f32[128,384]{1,0:T(8,128)}, u32[]{:S(2)}) copy-start(f32[128,384]{1,0:T(8,128)} %pad_maximum_fusion.6) | copy-start | bytes 589828
  1468.0 729.0 %all-to-all-start.1 = ((f32[8,128,8192]{2,1,0:T(8,128)}), f32[8,128,8192]{2,1,0:T(8,128)}, u32[]{:S(2)}, u32[]{:S(2)}) async-start(f32[8,128,8192]{2,1,0:T(8,128)} %bitcast.124), calls=%async_computation.1 | async-start | bytes 67108864 | tf_op jit(solution)/shard_map/all_to_all | solution.py:63
  1475.3 33.5 %copy-start.5 = (s32[65536]{0:T(1024)S(1)}, s32[65536]{0:T(1024)}, u32[]{:S(2)}) copy-start(s32[65536]{0:T(1024)} %param.9) | copy-start | bytes 786436
  1791.5 432.1 %copy-start.7 = (s32[128]{0:T(128)S(1)}, s32[128]{0:T(128)}, u32[]{:S(2)}) copy-start(s32[128]{0:T(128)} %param.10) | copy-start | bytes 1540
  2223.6 44.0 %copy-start.8 = (f32[128]{0:T(128)}, f32[128]{0:T(128)S(1)}, u32[]{:S(2)}) copy-start(f32[128]{0:T(128)S(1)} %add_sqrt_fusion) | copy-start | bytes 1540
Sparse Core Ops, SparseCore 0:
  1007.4 135.3 all-reduce.16
where the time goes:
time: 2290 us; the launch traced here: 2270 us
  blocking collectives  761 us (33%)
  waiting for transfers between devices  541 us (24%)
  local copies, waits for them, and re-layouts  519 us (23%)
  other arithmetic  266 us (12%)
  matrix products  165 us (7%)
    all_to_all x1, blocking collectives, local(): lax.all_to_all(pieces, 'band', split_axis=0, concat_axis=0, tiled=True)  735 us
    all_to_all x1, waiting for transfers between devices, local(): lax.all_to_all(ortho_cols.reshape(devices, bands, part), 'band', split_ax...  406 us
    gather x2, local copies, waits for them, and re-layouts, local(): jnp.take(ref_block, inverse, axis=1, unique_indices=True, mode='clip')  257 us
    psum x1, waiting for transfers between devices, local(): strips = lax.psum(jnp.concatenate(strips, axis=1), ('band', 'coef'))  135 us
    dot_general x8, matrix products, high(): jnp.dot(a, b, precision=lax.Precision.HIGH, preferred_element_type=jnp.fl...  134 us
    slice x9, local copies, waits for them, and re-layouts, local(): strips = [high(columns[t:t + ROWS], columns[:t + ROWS].T) for t in tops]  130 us
    another operation x24, other arithmetic, inverse_factor(): corner = lax.linalg.cholesky(rest[:BLOCK, :BLOCK], symmetrize_input=False)  99.4 us
    another operation x16, other arithmetic, inverse_factor(): inv = lax.linalg.triangular_solve(corner, eye, left_side=True, lower=True)  83.9 us
  transfers between devices with their start and end apart: 2, of which 2 were waited for; matrix products, arithmetic and copies ran while one was open for 14% of the time, Pallas kernels for 0%

commit v1 on v0

--- a/solution.py
+++ b/solution.py
@@ -6,6 +6,11 @@
 NGROUPS = 16
 BLOCK = 128
 ROWS = 256
+
+
+def gather_and_add(array, axis):
+    parts = lax.all_gather(array, axis)
+    return jnp.sum(parts, axis=0)
 
 
 def high(a, b):
@@ -47,7 +52,7 @@
     ref_own = jnp.take(ref_block, inverse, axis=1, unique_indices=True, mode="clip")
     tops = range(0, total, ROWS)
     strips = [high(columns[t : t + ROWS], columns[: t + ROWS].T) for t in tops]
-    strips = lax.psum(jnp.concatenate(strips, axis=1), ("band", "coef"))
+    strips = gather_and_add(jnp.concatenate(strips, axis=1), ("band", "coef"))
     lower, at = ([], 0)
     for t in tops:
         width = t + ROWS

time: 2290 us -> 2630 us (1.15)
  waiting for transfers between devices: 541 us -> 842 us
  other arithmetic: 266 us -> 300 us
    all_gather x0 -> x1, waiting for transfers between devices: none -> 435 us  [gather_and_add(): parts = lax.all_gather(array, axis)]
    psum x1 -> x0, waiting for transfers between devices: 135 us -> none  [local(): strips = lax.psum(jnp.concatenate(strips, axis=1), ('band', 'coef'))]
    unnamed x20 -> x24, local copies, waits for them, and re-layouts: 68.8 us -> 75.5 us
  transfers between devices with their start and end apart: 2 -> 2, of which waited for: 2 -> 2; matrix products, arithmetic and copies ran while one was open for 14% -> 12% of each run, Pallas kernels for 0% -> 0%
where the time goes in v1:
time: 2630 us; the launch traced here: 2620 us
  waiting for transfers between devices  842 us (32%)
  blocking collectives  761 us (29%)
  local copies, waits for them, and re-layouts  527 us (20%)
  other arithmetic  300 us (11%)
  matrix products  162 us (6%)
    all_to_all x1, blocking collectives, local(): lax.all_to_all(pieces, 'band', split_axis=0, concat_axis=0, tiled=True)  735 us
    all_gather x1, waiting for transfers between devices, gather_and_add(): parts = lax.all_gather(array, axis)  435 us
    all_to_all x1, waiting for transfers between devices, local(): lax.all_to_all(ortho_cols.reshape(devices, bands, part), 'band', split_ax...  407 us
    gather x2, local copies, waits for them, and re-layouts, local(): jnp.take(ref_block, inverse, axis=1, unique_indices=True, mode='clip')  257 us
    dot_general x8, matrix products, high(): jnp.dot(a, b, precision=lax.Precision.HIGH, preferred_element_type=jnp.fl...  131 us
    slice x9, local copies, waits for them, and re-layouts, local(): strips = [high(columns[t:t + ROWS], columns[:t + ROWS].T) for t in tops]  130 us
    another operation x24, other arithmetic, inverse_factor(): corner = lax.linalg.cholesky(rest[:BLOCK, :BLOCK], symmetrize_input=False)  99.5 us
    another operation x16, other arithmetic, inverse_factor(): inv = lax.linalg.triangular_solve(corner, eye, left_side=True, lower=True)  84.1 us
  transfers between devices with their start and end apart: 2, of which 2 were waited for; matrix products, arithmetic and copies ran while one was open for 12% of the time, Pallas kernels for 0%

profile of v1, /device:TPU:0, one launch (start us, length us, event | category | flops | bytes accessed | tf_op | source)
XLA Modules:
  0.0 2615.4 jit_solution(13440119646837093365)
XLA Ops:
  7.2 33.4 %copy.54 = f32[128,65536]{0,1:T(8,128)} copy(f32[128,65536]{1,0:T(8,128)} %param.7) | data formatting | bytes 67108864 | tf_op args[0]
  40.6 735.1 %all_to_all.10 = f32[8,128,8192]{1,2,0:T(8,128)} all-to-all(f32[8,128,8192]{1,2,0:T(8,128)} %bitcast.126), channel_id=1, replica_groups=mesh['band'=8,'coef'=4] {'band'}, dimensions={0} | all-to-all | bytes 67108864 | tf_op jit(solution)/shard_map/all_to_all | solution.py:49
  775.7 23.5 fusion.100
  808.2 16.9 slice.228
  825.1 24.7 copy.59
  870.1 17.5 copy.57
  905.4 14.1 fusion.102
  919.5 17.2 fusion.104
  936.7 13.7 fusion.103
  950.4 31.1 %copy.61 = f32[8,128,8192]{2,1,0:T(8,128)} copy(f32[8,128,8192]{1,2,0:T(8,128)} %all_to_all.10) | data formatting | bytes 67108864 | tf_op jit(solution)/shard_map/all_to_all | solution.py:49
  981.5 21.1 fusion.105
  1004.4 435.3 %all-gather.3.cloned.1.call-done = f32[8192,2560]{1,0:T(8,128)} async-done(((f32[256,2560]{1,0:T(8,128)}), f32[8192,2560]{1,0:T(8,128)}) %all-gather.3.cloned.1.call-update) | async-done | bytes 83886096 | tf_op jit(solution)/shard_map/all_gather | solution.py:12
  1439.7 26.0 reduce_sum.18
  1741.8 18.0 fusion.12
  1759.8 23.5 fusion.6
  1783.3 23.6 pad_maximum_fusion
  1814.2 33.4 %copy.77 = f32[128,65536]{0,1:T(8,128)} copy(f32[128,65536]{1,0:T(8,128)} %param.8) | data formatting | bytes 67108864 | tf_op args[1]
  1847.7 25.5 sort.15
  1873.2 226.1 %gather_fusion = f32[65536,128]{1,0:T(8,128)} fusion(f32[128,65536]{0,1:T(8,128)} %copy.77, s32[65536]{0:T(1024)S(1)} %broadcast_clamp_fusion), kind=kCustom, calls=%fused_computation | custom fusion | bytes 67371008 | tf_op jit(solution)/shard_map/jit(_take)/gather | solution.py:52
  2099.3 31.1 %copy.78 = f32[128,8,8192]{2,0,1:T(8,128)} copy(f32[128,8,8192]{0,2,1:T(8,128)} %bitcast.129) | data formatting | bytes 67108864 | tf_op jit(solution)/shard_map/jit(_take)/gather | solution.py:52
  2130.4 406.8 %all-to-all-done.1 = f32[8,128,8192]{2,1,0:T(8,128)} async-done(((f32[8,128,8192]{2,1,0:T(8,128)}), f32[8,128,8192]{2,1,0:T(8,128)}, u32[]{:S(2)}, u32[]{:S(2)}) %all-to-all-start.1) | async-done | bytes 33554464 | tf_op jit(solution)/shard_map/all_to_all | solution.py:68
  2537.2 20.9 fusion.1
  2564.5 20.2 psum.15
  2585.2 22.9 copy.85
  (149 shorter events, 338.2 us)
Async XLA Ops:
  7.2 1432.6 %all-gather.3.cloned.1.call-start = ((), (), s32[]{:S(2)}) async-start(), calls=%async_computation.2 | async-start | bytes 86507520 | tf_op jit(solution)/shard_map/all_gather | solution.py:12
  1465.8 10.1 copy-start.6
  1497.5 1.9 copy-start
  1558.1 1.5 copy-start.1
  1641.2 23.8 copy-start.2
  1693.1 35.4 %copy-start.3 = (f32[128,512]{1,0:T(8,128)S(1)}, f32[128,512]{1,0:T(8,128)}, u32[]{:S(2)}) copy-start(f32[128,512]{1,0:T(8,128)} %pad_maximum_fusion.5) | copy-start | bytes 786436
  1693.1 35.6 %copy-start.4 = (f32[128,384]{1,0:T(8,128)S(1)}, f32[128,384]{1,0:T(8,128)}, u32[]{:S(2)}) copy-start(f32[128,384]{1,0:T(8,128)} %pad_maximum_fusion.6) | copy-start | bytes 589828
  1806.9 730.3 %all-to-all-start.1 = ((f32[8,128,8192]{2,1,0:T(8,128)}), f32[8,128,8192]{2,1,0:T(8,128)}, u32[]{:S(2)}, u32[]{:S(2)}) async-start(f32[8,128,8192]{2,1,0:T(8,128)} %bitcast.125), calls=%async_computation.1 | async-start | bytes 67108864 | tf_op jit(solution)/shard_map/all_to_all | solution.py:68
  1814.2 33.5 %copy-start.5 = (s32[65536]{0:T(1024)S(1)}, s32[65536]{0:T(1024)}, u32[]{:S(2)}) copy-start(s32[65536]{0:T(1024)} %param.9) | copy-start | bytes 786436
  2130.4 433.9 %copy-start.7 = (s32[128]{0:T(128)S(1)}, s32[128]{0:T(128)}, u32[]{:S(2)}) copy-start(s32[128]{0:T(128)} %param.10) | copy-start | bytes 1540
  2564.3 43.8 %copy-start.8 = (f32[128]{0:T(128)}, f32[128]{0:T(128)S(1)}, u32[]{:S(2)}) copy-start(f32[128]{0:T(128)S(1)} %add_sqrt_fusion) | copy-start | bytes 1540
Sparse Core Ops, SparseCore 0:
  1004.6 435.1 all-gather.2
